TPU v7x, 512 devices: a whole 4x8x8 slice. The times are simulated.
512 devices in a mesh: elem: 32 (over y, x), mode: 16 (over z, core).
Axes of the slice: x: 4, y: 8, z: 8, core: 2. Of those that a mesh axis runs over, the one named last changes fastest.
Arguments:
- u_spec: bfloat16 [1024, 65536], P('mode', 'elem'), may hold values from -6 to 6
- dir_spec: bfloat16 [1024, 65536], P('mode', 'elem'), may hold values from -6 to 6
- advecting: bfloat16 [3, 1024, 65536], P(None, None, ('elem', 'mode')), may hold values from -6 to 6
- viscosity: bfloat16 [1024, 65536], P(None, ('elem', 'mode')), may hold values from 0.099609375 to 2
- degrees: int32 [2, 1024], P(None, 'elem'), may hold values from 2 to 7
- edge_side: int32 [4096], P('elem'), may hold values from 0 to 127, as said below
- edge_link: int32 [3, 4096], P(None, 'elem'), may hold values from -1 to 127, as said below
Outputs:
- advect: float32 [1024, 65536], P('mode', 'elem')
- helm_velocity: float32 [1024, 65536], P('mode', 'elem')
- helm_direction: float32 [1024, 65536], P('mode', 'elem')
Inputs may be any that keep to these rules, and one draw needn't show every extreme that they name: `edge_side`: within each partition's 128 slots, no element side appears twice. `edge_link`: A slot with peer -1 is empty and has flag 0 and peer slot 0. Pairing is symmetric: a live slot's partner is live, names it back and has the same flag. A peer is the partition itself (another slot) or a partition one or two places away around the closed loop of 32 partitions. At most 24 live slots of one partition name any one other partition as peer, and some partition has exactly that many with each of its four neighbours. Some partition has all 128 slots live.
All inputs are finite; a program needn't handle non-finite values.
Results may differ from a plain program's by a relative error of at most 0.0055.
Values may be sent and summed in bfloat16 or wider, within the bound.
A program may use at most 128 MiB of HBM per device.

v0:
```python
import math

import jax
import jax.numpy as jnp
import ml_dtypes
import numpy as np
from jax import lax
from jax.experimental import pallas as pl
from jax.experimental.pallas import tpu as pltpu
from jax.sharding import PartitionSpec as P

METRIC = 0.125
AREA_SCALE = 64.0
LENGTH = 8.0
HELM_LAMBDA = 4.0
PENALTY = 0.02
OFFSETS = (1, 2, -1, -2)
NEAR = 24
LANES = 128
F32 = jnp.float32
BF16 = jnp.bfloat16


def cheb_tables():
    top = 7
    angles = np.pi * np.arange(top + 1) / top
    points = np.cos(angles)
    scale = np.ones(top + 1)
    scale[0] = 2.0
    scale[top] = 2.0
    scale = scale * (-1.0) ** np.arange(top + 1)
    differences = points[:, None] - points[None, :]
    derivative = scale[:, None] / scale[None, :] / (differences + np.eye(top + 1))
    derivative = derivative - np.eye(top + 1) * derivative.sum(axis=1)[:, None]
    weights = np.zeros(top + 1)
    interior = np.ones(top - 1)
    for k in range(1, (top - 1) // 2 + 1):
        interior = interior - 2.0 * np.cos(2 * k * angles[1:top]) / (4 * k * k - 1)
    weights[0] = 1.0 / (top * top)
    weights[top] = weights[0]
    weights[1:top] = 2.0 * interior / top
    return derivative, weights


def synthesis_table(total):
    planes = np.arange(total)
    turns = planes[:, None] * (planes // 2)[None, :] % total
    angles = 2.0 * np.pi / total * turns
    table = np.where((planes % 2)[None, :] == 0, np.cos(angles), np.sin(angles))
    table = table * math.sqrt(2.0 / total)
    table[:, 0] = 1.0 / math.sqrt(total)
    table[:, 1] = (1 - 2 * (planes % 2)) / math.sqrt(total)
    return table.astype(np.float32).astype(ml_dtypes.bfloat16)


def operator_tables(block_elements):
    derivative, weights = cheb_tables()
    eye8 = np.eye(8)
    eye_block = np.eye(block_elements)
    kron_x = np.kron(np.kron(METRIC * derivative, eye8), eye_block).astype(np.float32)
    kron_y = np.kron(np.kron(eye8, METRIC * derivative), eye_block).astype(np.float32)

    def halves(matrix):
        high = matrix.astype(ml_dtypes.bfloat16)
        low = (matrix - high.astype(np.float32)).astype(ml_dtypes.bfloat16)
        return np.concatenate([high, high, low], axis=0)

    forward = halves(np.concatenate([kron_x.T, kron_y.T], axis=1))
    backward = halves(np.concatenate([kron_x, kron_y], axis=0))
    mass = np.repeat(AREA_SCALE * np.outer(weights, weights).reshape(-1), block_elements)
    return forward, backward, mass.astype(np.float32)[None, :]


def split_dot(values, stacked):
    high = values.astype(BF16)
    low = (values - high.astype(F32)).astype(BF16)
    return jnp.dot(
        jnp.concatenate([high, low, high], axis=1), stacked, preferred_element_type=F32
    )


def span_slope(values, first_row, total):
    rows = values.shape[0]
    row = lax.broadcasted_iota(jnp.int32, values.shape, 0)
    rate = (4.0 / total) * ((row + first_row) >> 1).astype(F32)
    above = pltpu.roll(values, rows - 1, 0)
    below = pltpu.roll(values, 1, 0)
    return rate * jnp.where((row & 1) == 0, above, -below)


def planes_kernel(
    coeff_ref, adv_ref, visc_ref, syn_ref, fwd_ref, bwd_ref, mass_ref, out_ref, stack, back
):
    blocks, _, rows, width = coeff_ref.shape
    total = blocks * rows
    for b in range(blocks):
        for f in range(2):
            values = coeff_ref[b, f]
            span = pl.ds(b * rows, rows)
            stack[span, pl.ds(2 * f * width, width)] = values
            stack[span, pl.ds((2 * f + 1) * width, width)] = span_slope(
                values.astype(F32), b * rows, total
            ).astype(BF16)
    chunk = 256
    for c in range(total // chunk):
        span = pl.ds(c * chunk, chunk)
        phys = jnp.dot(syn_ref[span, :], stack[...], preferred_element_type=F32)
        weighted = mass_ref[...] * visc_ref[span, :].astype(F32)
        for f in range(2):
            plain = phys[:, 2 * f * width : (2 * f + 1) * width]
            along = phys[:, (2 * f + 1) * width : (2 * f + 2) * width]
            grads = split_dot(plain, fwd_ref[...])
            grad_x = grads[:, :width]
            grad_y = grads[:, width:]
            if f == 0:
                moved = (
                    adv_ref[0, span, :].astype(F32) * grad_x
                    + adv_ref[1, span, :].astype(F32) * grad_y
                    + adv_ref[2, span, :].astype(F32) * along
                )
                back[span, pl.ds(0, width)] = moved.astype(BF16)
            flat = split_dot(
                jnp.concatenate([weighted * grad_x, weighted * grad_y], axis=1), bwd_ref[...]
            )
            back[span, pl.ds((2 * f + 1) * width, width)] = flat.astype(BF16)
            back[span, pl.ds((2 * f + 2) * width, width)] = (weighted * along).astype(BF16)
    for c in range(total // chunk):
        spec = lax.dot_general(
            syn_ref[:, pl.ds(c * chunk, chunk)],
            back[...],
            (((0,), (0,)), ((), ())),
            preferred_element_type=F32,
        )
        for f in range(3):
            part = spec[:, :width]
            if f > 0:
                low = (2 * f - 1) * width
                part = spec[:, low : low + width] - span_slope(
                    spec[:, low + width : low + 2 * width], c * chunk, total
                )
            part = part.astype(BF16)
            for b in range(chunk // rows):
                out_ref[c * (chunk // rows) + b, f] = part[b * rows : (b + 1) * rows]


def split_kernel(u_ref, d_ref, out_ref):
    width = out_ref.shape[3]
    for b in range(out_ref.shape[0]):
        span = pl.ds(b * width, width)
        out_ref[b, 0] = u_ref[:, span]
        out_ref[b, 1] = d_ref[:, span]


class SlotTables:
    def __init__(self, deg_ref, side_ref, link_ref):
        slots = side_ref.shape[1]
        self.slots = slots
        self.sub = lax.broadcasted_iota(jnp.int32, (slots, slots), 0)
        self.lane = lax.broadcasted_iota(jnp.int32, (slots, slots), 1)
        self.eye = self.sub == self.lane
        side = side_ref[...]
        element = side >> 2
        code = side & 3
        start = jnp.where(code == 0, 0, jnp.where(code == 1, 7, jnp.where(code == 2, 63, 56)))
        step = jnp.where(code == 0, 1, jnp.where(code == 1, 8, jnp.where(code == 2, -1, -8)))
        first = (element >> 1) * LANES + (element & 1) + 2 * start
        self.first_row = first.astype(F32)
        self.step_row = (2 * step).astype(F32)
        self.flip_row = link_ref[0:1, :].astype(F32)
        self.peer_row = link_ref[1:2, :].astype(F32)
        self.slot_row = link_ref[2:3, :].astype(F32)
        element_col = self.column(element.astype(F32))
        code_col = self.column((code & 1).astype(F32))
        count = deg_ref.shape[1]
        member = lax.broadcasted_iota(jnp.int32, (slots, count), 1).astype(F32) == element_col
        degree = jnp.where(
            code_col == 0.0, deg_ref[0:1, :].astype(F32), deg_ref[1:2, :].astype(F32)
        )
        self.degree_col = jnp.sum(jnp.where(member, degree, 0.0), axis=1, keepdims=True)
        self.degree_row = jnp.sum(
            jnp.where(self.eye, self.degree_col, 0.0), axis=0, keepdims=True
        )
        self.peer_col = self.column(self.peer_row)

    def column(self, row):
        return jnp.sum(jnp.where(self.eye, row, 0.0), axis=1, keepdims=True)

    def peer_of(self, offset):
        parts = lax.axis_size("elem")
        return ((lax.axis_index("elem") + offset + parts) % parts).astype(F32)

    def chosen(self, offset, before):
        peer = self.peer_of(offset)
        ahead = jnp.where((self.peer_col == peer) & before, 1.0, 0.0)
        place = jnp.sum(ahead, axis=0, keepdims=True)
        order = lax.broadcasted_iota(jnp.int32, (NEAR, self.slots), 0).astype(F32)
        return jnp.where((self.peer_row == peer) & (place == order), 1.0, 0.0)


def trace_kernel(u_ref, d_ref, deg_ref, side_ref, link_ref, trace_ref, packed_ref):
    tables = SlotTables(deg_ref, side_ref, link_ref)
    columns = u_ref.shape[1]
    values = jnp.concatenate([u_ref[...], d_ref[...]], axis=0)
    before = tables.sub < tables.lane
    picks = [tables.chosen(offset, before) for offset in OFFSETS]
    picks_all = jnp.concatenate(picks, axis=0).astype(BF16)
    first_col = tables.column(tables.first_row)
    step_col = tables.column(tables.step_row)
    ids = lax.broadcasted_iota(jnp.int32, (tables.slots, columns), 1)
    nt = (((1,), (1,)), ((), ()))
    for k in range(8):
        wanted = (first_col + step_col * float(k)).astype(jnp.int32)
        hot = jnp.where(ids == wanted, 1.0, 0.0).astype(BF16)
        trace = lax.dot_general(values, hot, nt, preferred_element_type=F32).astype(BF16)
        trace_ref[k] = trace
        packed = lax.dot_general(picks_all, trace, nt, preferred_element_type=F32)
        for o in range(4):
            packed_ref[o, k] = packed[o * NEAR : (o + 1) * NEAR].astype(BF16)
    for o in range(4):
        degree = jnp.sum(picks[o] * tables.degree_row, axis=1, keepdims=True)
        packed_ref[o, 8] = jnp.broadcast_to(degree, (NEAR, LANES)).astype(BF16)


def penalty_kernel(
    edge_weight,
    u_ref,
    d_ref,
    deg_ref,
    side_ref,
    link_ref,
    mass_ref,
    trace_ref,
    near0,
    near1,
    near2,
    near3,
    out_ref,
    left,
):
    nears = (near0, near1, near2, near3)
    tables = SlotTables(deg_ref, side_ref, link_ref)
    rows, columns = u_ref.shape
    slot_col = tables.column(tables.slot_row)

    def aims(match, other_degree):
        def pick(row):
            return jnp.sum(match * row, axis=1, keepdims=True)

        alive = pick(jnp.ones_like(tables.degree_row))
        return alive, pick(tables.first_row), pick(tables.step_row), pick(
            tables.degree_row
        ), other_degree

    mine = tables.peer_of(0)
    match = jnp.where(
        (tables.peer_col == mine) & (slot_col == tables.lane.astype(F32)), 1.0, 0.0
    )
    flips = [tables.column(tables.flip_row)]
    sets = [aims(match, tables.degree_col)]
    before = slot_col < tables.slot_row
    for o, offset in enumerate(OFFSETS):
        match = tables.chosen(offset, before)
        flips.append(jnp.sum(match * tables.flip_row, axis=1, keepdims=True))
        sets.append(aims(match, nears[o][8].astype(F32)[:, 0:1]))
    filler = 2 * LANES - tables.slots - 4 * NEAR
    zeros = jnp.zeros((filler, 1), F32)

    def joined(parts):
        return jnp.concatenate(list(parts) + [zeros], axis=0)

    alive = joined(s[0] for s in sets)
    first = joined(s[1] for s in sets)
    step = joined(s[2] for s in sets)
    degree = jnp.maximum(joined(s[3] for s in sets), joined(s[4] for s in sets))
    flip = joined(flips)
    first = jnp.where(alive > 0.0, first + 7.0 * flip * step, -1.0e6)
    step = step * (1.0 - 2.0 * flip)
    strength = alive * PENALTY * (degree + 1.0) * (degree + 1.0)
    for k in range(8):
        received = jnp.concatenate(
            [near[k].astype(F32) for near in nears] + [jnp.zeros((filler, LANES), F32)], axis=0
        )
        left[pl.ds(0, LANES), pl.ds(k * 2 * LANES, LANES)] = trace_ref[k]
        left[pl.ds(0, LANES), pl.ds((k * 2 + 1) * LANES, LANES)] = received.T.astype(BF16)
    left[pl.ds(LANES, 16), :] = jnp.ones((16, left.shape[1]), BF16)
    wide = 256
    ids = lax.broadcasted_iota(jnp.int32, (2 * LANES, wide), 1)
    targets = [(first + step * float(k)).astype(jnp.int32) for k in range(8)]
    factors = [strength * float(edge_weight[k]) for k in range(8)]
    mass = HELM_LAMBDA * jnp.concatenate([mass_ref[...]] * (wide // LANES), axis=1)
    for c in range(columns // wide):
        hot = jnp.concatenate(
            [
                jnp.where(ids == targets[k] - c * wide, factors[k], 0.0).astype(BF16)
                for k in range(8)
            ],
            axis=0,
        )
        summed = jnp.dot(left[...], hot, preferred_element_type=F32)
        scale = mass + summed[LANES : LANES + 1, :]
        span = pl.ds(c * wide, wide)
        out_ref[0, :, span] = scale * u_ref[:, span].astype(F32) - summed[:rows]
        out_ref[1, :, span] = scale * d_ref[:, span].astype(F32) - summed[rows : 2 * rows]


def final_kernel(back_ref, local_ref, adv_ref, vel_ref, dir_ref):
    width = back_ref.shape[3]
    for b in range(back_ref.shape[0]):
        span = pl.ds(b * width, width)
        adv_ref[:, span] = back_ref[b, 0].astype(F32)
        vel_ref[:, span] = local_ref[0, :, span] + back_ref[b, 1].astype(F32)
        dir_ref[:, span] = local_ref[1, :, span] + back_ref[b, 2].astype(F32)


def call(kernel, outs, name, scratch=(), cost=None):
    return pl.pallas_call(
        kernel,
        out_shape=outs,
        scratch_shapes=list(scratch),
        name=name,
        cost_estimate=cost,
        compiler_params=pltpu.CompilerParams(vmem_limit_bytes=48 * 1024 * 1024),
    )


def cost(flops, moved):
    return pl.CostEstimate(flops=flops, bytes_accessed=moved, transcendentals=0)


def on_device(u_spec, dir_spec, advecting, viscosity, degrees, edge_side, edge_link):
    shape = jax.ShapeDtypeStruct
    modes = lax.axis_size("mode")
    total, width = viscosity.shape
    rows, columns = u_spec.shape
    forward, backward, mass = operator_tables(degrees.shape[1] // modes)
    weights = LENGTH * cheb_tables()[1]
    side = edge_side[None, :]
    slots = edge_side.shape[0]

    sent = call(split_kernel, shape((modes, 2, rows, width), BF16), "split")(u_spec, dir_spec)
    coeffs = lax.all_to_all(sent, "mode", split_axis=0, concat_axis=0, tiled=True)

    traces, packed = call(
        trace_kernel,
        (shape((8, 2 * rows, slots), BF16), shape((4, 9, NEAR, LANES), BF16)),
        "trace",
        cost=cost(1 << 29, 1 << 20),
    )(u_spec, dir_spec, degrees, side, edge_link)
    parts = lax.axis_size("elem")
    nears = [
        lax.ppermute(packed[o], "elem", [((i + offset) % parts, i) for i in range(parts)])
        for o, offset in enumerate((-d for d in OFFSETS))
    ]
    nears = [nears[2], nears[3], nears[0], nears[1]]
    local = call(
        lambda *refs: penalty_kernel(weights, *refs),
        shape((2, rows, columns), F32),
        "penalty",
        scratch=[pltpu.VMEM((LANES + 16, 16 * LANES), BF16)],
        cost=cost(1 << 30, 1 << 21),
    )(u_spec, dir_spec, degrees, side, edge_link, mass, traces, *nears)

    returned = call(
        planes_kernel,
        shape((modes, 3, rows, width), BF16),
        "planes",
        scratch=[pltpu.VMEM((total, 4 * width), BF16), pltpu.VMEM((total, 5 * width), BF16)],
        cost=cost(1 << 32, 1 << 22),
    )(coeffs, advecting, viscosity, synthesis_table(total), forward, backward, mass)
    volumes = lax.all_to_all(returned, "mode", split_axis=0, concat_axis=0, tiled=True)
    out = shape((rows, columns), F32)
    return call(final_kernel, (out, out, out), "final")(volumes, local)


def solution(mesh):
    in_specs = (
        P("mode", "elem"),
        P("mode", "elem"),
        P(None, None, ("elem", "mode")),
        P(None, ("elem", "mode")),
        P(None, "elem"),
        P("elem"),
        P(None, "elem"),
    )
    out_specs = (P("mode", "elem"), P("mode", "elem"), P("mode", "elem"))
    return jax.shard_map(
        on_device, mesh=mesh, in_specs=in_specs, out_specs=out_specs, check_vma=False
    )
```

profile of v0, /device:TPU:30, one launch (start us, length us, event | category | flops | bytes accessed | tf_op | source)
XLA Modules:
  0.0 70.8 jit_solution(8079834347430137575)
XLA Ops:
  0.6 0.0 copy-start.12
  0.6 0.0 copy-start
  0.7 0.9 %copy-done = bf16[64,2048]{1,0:T(8,128)(2,1)S(1)} copy-done((bf16[64,2048]{1,0:T(8,128)(2,1)S(1)}, bf16[64,2048]{1,0:T(8,128)(2,1)}, u32[]{:S(2)}) %copy-start) | copy-done | bytes 262168
  1.6 0.0 copy-start.2
  1.6 0.9 %copy-done.2 = bf16[64,2048]{1,0:T(8,128)(2,1)S(1)} copy-done((bf16[64,2048]{1,0:T(8,128)(2,1)S(1)}, bf16[64,2048]{1,0:T(8,128)(2,1)}, u32[]{:S(2)}) %copy-start.2) | copy-done | bytes 262168
  2.6 0.0 copy-start.4
  2.6 0.0 copy-start.5
  2.6 0.0 copy-start.10
  2.6 0.0 copy-start.11
  2.6 0.1 split.1
  2.7 26.3 %all_to_all.10.coeff_ref = bf16[16,2,64,128]{3,2,1,0:T(8,128)(2,1)S(1)} all-to-all(bf16[16,2,64,128]{3,2,1,0:T(8,128)(2,1)S(1)} %split.1), channel_id=1, replica_groups=mesh['elem'=32,'mode'=16] {'mode'}, dimensions={0} | all-to-all | bytes 1048576 | tf_op jit(solution)/shard_map/all_to_all | solution.py:341
  29.0 0.0 copy-done.12
  29.0 0.0 copy-done.4
  29.0 0.0 copy-done.5
  29.0 0.0 copy-done.10
  29.0 0.0 copy-done.11
  29.0 0.0 copy-start.9
  29.0 1.6 %copy-done.9 = bf16[1024,1024]{1,0:T(8,128)(2,1)S(1)} copy-done((bf16[1024,1024]{1,0:T(8,128)(2,1)S(1)}, bf16[1024,1024]{1,0:T(8,128)(2,1)}, u32[]{:S(2)}) %copy-start.9) | copy-done | bytes 2097176
  30.6 0.0 copy-start.1
  30.6 0.0 copy-start.3
  30.6 0.0 copy-start.6
  30.6 0.0 copy-start.7
  30.6 0.0 copy-start.8
  30.6 7.1 %planes.1 = bf16[16,3,64,128]{3,2,1,0:T(8,128)(2,1)} custom-call(bf16[16,2,64,128]{3,2,1,0:T(8,128)(2,1)S(1)} %all_to_all.10.coeff_ref, bf16[3,1024,128]{2,1,0:T(8,128)(2,1)S(1)} %copy-done.4, bf16[1024,128]{1,0:T(8,128)(2,1)S(1)} %copy-done.5, bf16[1024,1024]{1,0:T(8,128)(2,1)S(1)} %copy-done.9, bf16[384,256]{1,0:T(8,128)(2,1)S(1)} %copy-done.11, ...), custom_call_target="tpu_custom_call" | custom-call | flops 4294967296 | bytes 4194304 | tf_op jit(solution)/shard_map/planes/pallas_call | solution.py:363
  37.7 4.2 %all-to-all-start.1 = ((bf16[16,3,64,128]{3,2,1,0:T(8,128)(2,1)}), bf16[16,3,64,128]{3,2,1,0:T(8,128)(2,1)S(1)}, u32[]{:S(2)}, u32[]{:S(2)}) async-start(bf16[16,3,64,128]{3,2,1,0:T(8,128)(2,1)} %planes.1), calls=%async_computation.1 | async-start | bytes 1572864 | tf_op jit(solution)/shard_map/all_to_all | solution.py:370
  42.0 0.0 copy-done.1
  42.0 0.0 copy-done.3
  42.0 0.0 copy-done.6
  42.0 0.0 copy-done.7
  42.0 0.0 copy-done.8
  42.0 3.7 %trace.1 = (bf16[8,128,128]{2,1,0:T(8,128)(2,1)S(1)}, bf16[4,9,24,128]{3,2,1,0:T(8,128)(2,1)S(1)}) custom-call(bf16[64,2048]{1,0:T(8,128)(2,1)S(1)} %copy-done.1, bf16[64,2048]{1,0:T(8,128)(2,1)S(1)} %copy-done.3, s32[2,32]{1,0:T(2,128)S(1)} %copy-done.7, s32[1,128]{1,0:T(1,128)S(1)} %bitcast.9, s32[3,128]{1,0:T(4,128)S(1)} %copy-done.6), custom_call_target="tpu_custom_call" | custom-call | flops 536870912 | bytes 1048576 | tf_op jit(solution)/shard_map/trace/pallas_call | solution.py:343
  45.7 5.5 %collective-permute-start.3 = (bf16[9,24,128]{2,1,0:T(8,128)(2,1)S(1)}, bf16[9,24,128]{2,1,0:T(8,128)(2,1)S(1)}, u32[]{:S(2)}, u32[]{:S(2)}) collective-permute-start(bf16[9,24,128]{2,1,0:T(8,128)(2,1)S(1)} %get-tuple-element.7), channel_id=1, source_target_pairs={{480,0},{496,16},{0,32},{16,48},{32,64},{48,80},{64,96},{80,112},{... | collective-permute-start | bytes 165896 | tf_op jit(solution)/shard_map/ppermute | solution.py:351
  51.3 4.0 %collective-permute-start.2 = (bf16[9,24,128]{2,1,0:T(8,128)(2,1)S(1)}, bf16[9,24,128]{2,1,0:T(8,128)(2,1)S(1)}, u32[]{:S(2)}, u32[]{:S(2)}) collective-permute-start(bf16[9,24,128]{2,1,0:T(8,128)(2,1)S(1)} %get-tuple-element.8), channel_id=1, source_target_pairs={{496,0},{0,16},{16,32},{32,48},{48,64},{64,80},{80,96},{96,112},{1... | collective-permute-start | bytes 165896 | tf_op jit(solution)/shard_map/ppermute | solution.py:351
  55.3 1.9 %collective-permute-start.1 = (bf16[9,24,128]{2,1,0:T(8,128)(2,1)S(1)}, bf16[9,24,128]{2,1,0:T(8,128)(2,1)S(1)}, u32[]{:S(2)}, u32[]{:S(2)}) collective-permute-start(bf16[9,24,128]{2,1,0:T(8,128)(2,1)S(1)} %get-tuple-element.9), channel_id=1, source_target_pairs={{32,0},{48,16},{64,32},{80,48},{96,64},{112,80},{128,96},{144,112}... | collective-permute-start | bytes 165896 | tf_op jit(solution)/shard_map/ppermute | solution.py:351
  57.2 1.9 %collective-permute-start = (bf16[9,24,128]{2,1,0:T(8,128)(2,1)S(1)}, bf16[9,24,128]{2,1,0:T(8,128)(2,1)S(1)}, u32[]{:S(2)}, u32[]{:S(2)}) collective-permute-start(bf16[9,24,128]{2,1,0:T(8,128)(2,1)S(1)} %get-tuple-element.10), channel_id=1, source_target_pairs={{16,0},{32,16},{48,32},{64,48},{80,64},{96,80},{112,96},{128,112},... | collective-permute-start | bytes 165896 | tf_op jit(solution)/shard_map/ppermute | solution.py:351
  59.1 0.0 collective-permute-done.3.refs_10_
  59.2 0.0 collective-permute-done.2.refs_9_
  59.2 5.9 %collective-permute-done.1.refs_8_ = bf16[9,24,128]{2,1,0:T(8,128)(2,1)S(1)} collective-permute-done((bf16[9,24,128]{2,1,0:T(8,128)(2,1)S(1)}, bf16[9,24,128]{2,1,0:T(8,128)(2,1)S(1)}, u32[]{:S(2)}, u32[]{:S(2)}) %collective-permute-start.1) | collective-permute-done | bytes 55328 | tf_op jit(solution)/shard_map/ppermute | solution.py:351
  65.1 1.5 %collective-permute-done.refs_7_ = bf16[9,24,128]{2,1,0:T(8,128)(2,1)S(1)} collective-permute-done((bf16[9,24,128]{2,1,0:T(8,128)(2,1)S(1)}, bf16[9,24,128]{2,1,0:T(8,128)(2,1)S(1)}, u32[]{:S(2)}, u32[]{:S(2)}) %collective-permute-start) | collective-permute-done | bytes 55328 | tf_op jit(solution)/shard_map/ppermute | solution.py:351
  66.6 2.9 %penalty.1.local_ref = f32[2,64,2048]{2,1,0:T(8,128)S(1)} custom-call(bf16[64,2048]{1,0:T(8,128)(2,1)S(1)} %copy-done.1, bf16[64,2048]{1,0:T(8,128)(2,1)S(1)} %copy-done.3, s32[2,32]{1,0:T(2,128)S(1)} %copy-done.7, s32[1,128]{1,0:T(1,128)S(1)} %bitcast.10, s32[3,128]{1,0:T(4,128)S(1)} %copy-done.6, f32[1,128]{1,0:T(1,128)S(1)} %copy-done.12, ...), custom_call_target="tpu_custom_call" | custom-call | flops 1073741824 | bytes 2097152 | tf_op jit(solution)/shard_map/penalty/pallas_call | solution.py:355
  69.5 0.0 all-to-all-done.1.back_ref
  69.5 1.3 %final.1 = (f32[64,2048]{1,0:T(8,128)}, f32[64,2048]{1,0:T(8,128)}, f32[64,2048]{1,0:T(8,128)}) custom-call(bf16[16,3,64,128]{3,2,1,0:T(8,128)(2,1)S(1)} %all-to-all-done.1.back_ref, f32[2,64,2048]{2,1,0:T(8,128)S(1)} %penalty.1.local_ref), custom_call_target="tpu_custom_call" | custom-call | tf_op jit(solution)/shard_map/final/pallas_call | solution.py:372
  (1 shorter events, 0.0 us)
Async XLA Ops:
  0.6 28.3 %copy-start.12 = (f32[1,128]{1,0:T(1,128)S(1)}, f32[1,128]{1,0:T(1,128)}, u32[]{:S(2)}) copy-start(f32[1,128]{1,0:T(1,128)} %constant.8.clone.mass_ref.refs_5_) | copy-start | bytes 1540
  0.6 1.0 %copy-start = (bf16[64,2048]{1,0:T(8,128)(2,1)S(1)}, bf16[64,2048]{1,0:T(8,128)(2,1)}, u32[]{:S(2)}) copy-start(bf16[64,2048]{1,0:T(8,128)(2,1)} %refs_0_.1) | copy-start | bytes 786436
  1.6 0.9 %copy-start.2 = (bf16[64,2048]{1,0:T(8,128)(2,1)S(1)}, bf16[64,2048]{1,0:T(8,128)(2,1)}, u32[]{:S(2)}) copy-start(bf16[64,2048]{1,0:T(8,128)(2,1)} %refs_1_.1) | copy-start | bytes 786436
  2.6 26.4 %copy-start.4 = (bf16[3,1024,128]{2,1,0:T(8,128)(2,1)S(1)}, bf16[3,1024,128]{2,1,0:T(8,128)(2,1)}, u32[]{:S(2)}) copy-start(bf16[3,1024,128]{2,1,0:T(8,128)(2,1)} %adv_ref.1) | copy-start | bytes 2359300
  2.6 26.4 %copy-start.5 = (bf16[1024,128]{1,0:T(8,128)(2,1)S(1)}, bf16[1024,128]{1,0:T(8,128)(2,1)}, u32[]{:S(2)}) copy-start(bf16[1024,128]{1,0:T(8,128)(2,1)} %visc_ref.1) | copy-start | bytes 786436
  2.6 26.4 %copy-start.10 = (bf16[768,128]{1,0:T(8,128)(2,1)S(1)}, bf16[768,128]{1,0:T(8,128)(2,1)}, u32[]{:S(2)}) copy-start(bf16[768,128]{1,0:T(8,128)(2,1)} %constant.11.clone.bwd_ref) | copy-start | bytes 589828
  2.6 26.4 %copy-start.11 = (bf16[384,256]{1,0:T(8,128)(2,1)S(1)}, bf16[384,256]{1,0:T(8,128)(2,1)}, u32[]{:S(2)}) copy-start(bf16[384,256]{1,0:T(8,128)(2,1)} %constant.10.clone.fwd_ref) | copy-start | bytes 589828
  29.0 1.6 %copy-start.9 = (bf16[1024,1024]{1,0:T(8,128)(2,1)S(1)}, bf16[1024,1024]{1,0:T(8,128)(2,1)}, u32[]{:S(2)}) copy-start(bf16[1024,1024]{1,0:T(8,128)(2,1)} %constant.9.clone.syn_ref) | copy-start | bytes 6291460
  30.6 11.4 %copy-start.1 = (bf16[64,2048]{1,0:T(8,128)(2,1)S(1)}, bf16[64,2048]{1,0:T(8,128)(2,1)}, u32[]{:S(2)}) copy-start(bf16[64,2048]{1,0:T(8,128)(2,1)} %refs_0_.1) | copy-start | bytes 786436
  30.6 11.4 %copy-start.3 = (bf16[64,2048]{1,0:T(8,128)(2,1)S(1)}, bf16[64,2048]{1,0:T(8,128)(2,1)}, u32[]{:S(2)}) copy-start(bf16[64,2048]{1,0:T(8,128)(2,1)} %refs_1_.1) | copy-start | bytes 786436
  30.6 11.4 %copy-start.6 = (s32[3,128]{1,0:T(4,128)S(1)}, s32[3,128]{1,0:T(4,128)}, u32[]{:S(2)}) copy-start(s32[3,128]{1,0:T(4,128)} %refs_4_.1) | copy-start | bytes 4612
  30.6 11.4 %copy-start.7 = (s32[2,32]{1,0:T(2,128)S(1)}, s32[2,32]{1,0:T(2,128)}, u32[]{:S(2)}) copy-start(s32[2,32]{1,0:T(2,128)} %refs_2_.1) | copy-start | bytes 772
  30.6 11.4 %copy-start.8 = (s32[128]{0:T(128)S(1)}, s32[128]{0:T(128)}, u32[]{:S(2)}) copy-start(s32[128]{0:T(128)} %param.16) | copy-start | bytes 1540
  37.7 31.8 %all-to-all-start.1 = ((bf16[16,3,64,128]{3,2,1,0:T(8,128)(2,1)}), bf16[16,3,64,128]{3,2,1,0:T(8,128)(2,1)S(1)}, u32[]{:S(2)}, u32[]{:S(2)}) async-start(bf16[16,3,64,128]{3,2,1,0:T(8,128)(2,1)} %planes.1), calls=%async_computation.1 | async-start | bytes 1572864 | tf_op jit(solution)/shard_map/all_to_all | solution.py:370
  45.7 13.4 %collective-permute-start.3 = (bf16[9,24,128]{2,1,0:T(8,128)(2,1)S(1)}, bf16[9,24,128]{2,1,0:T(8,128)(2,1)S(1)}, u32[]{:S(2)}, u32[]{:S(2)}) collective-permute-start(bf16[9,24,128]{2,1,0:T(8,128)(2,1)S(1)} %get-tuple-element.7), channel_id=1, source_target_pairs={{480,0},{496,16},{0,32},{16,48},{32,64},{48,80},{64,96},{80,112},{... | collective-permute-start | bytes 165896 | tf_op jit(solution)/shard_map/ppermute | solution.py:351
  51.3 7.9 %collective-permute-start.2 = (bf16[9,24,128]{2,1,0:T(8,128)(2,1)S(1)}, bf16[9,24,128]{2,1,0:T(8,128)(2,1)S(1)}, u32[]{:S(2)}, u32[]{:S(2)}) collective-permute-start(bf16[9,24,128]{2,1,0:T(8,128)(2,1)S(1)} %get-tuple-element.8), channel_id=1, source_target_pairs={{496,0},{0,16},{16,32},{32,48},{48,64},{64,80},{80,96},{96,112},{1... | collective-permute-start | bytes 165896 | tf_op jit(solution)/shard_map/ppermute | solution.py:351
  55.3 9.8 %collective-permute-start.1 = (bf16[9,24,128]{2,1,0:T(8,128)(2,1)S(1)}, bf16[9,24,128]{2,1,0:T(8,128)(2,1)S(1)}, u32[]{:S(2)}, u32[]{:S(2)}) collective-permute-start(bf16[9,24,128]{2,1,0:T(8,128)(2,1)S(1)} %get-tuple-element.9), channel_id=1, source_target_pairs={{32,0},{48,16},{64,32},{80,48},{96,64},{112,80},{128,96},{144,112}... | collective-permute-start | bytes 165896 | tf_op jit(solution)/shard_map/ppermute | solution.py:351
  57.2 9.4 %collective-permute-start = (bf16[9,24,128]{2,1,0:T(8,128)(2,1)S(1)}, bf16[9,24,128]{2,1,0:T(8,128)(2,1)S(1)}, u32[]{:S(2)}, u32[]{:S(2)}) collective-permute-start(bf16[9,24,128]{2,1,0:T(8,128)(2,1)S(1)} %get-tuple-element.10), channel_id=1, source_target_pairs={{16,0},{32,16},{48,32},{64,48},{80,64},{96,80},{112,96},{128,112},... | collective-permute-start | bytes 165896 | tf_op jit(solution)/shard_map/ppermute | solution.py:351
where the time goes:
time: 71.2 us; the launch traced here: 70.8 us
  blocking collectives  26.3 us (37%)
  starting transfers between devices  17.6 us (25%)
  Pallas kernels  15 us (21%)
  waiting for transfers between devices  7.43 us (10%)
  local copies, waits for them, and re-layouts  3.55 us (5%)
  between operations  0.83 us (1%)
    all_to_all x1, blocking collectives, on_device(): lax.all_to_all(sent, 'mode', split_axis=0, concat_axis=0, tiled=True)  26.3 us
    ppermute x4, starting transfers between devices, on_device(): lax.ppermute(packed[o], 'elem', [((i + offset) % parts, i) for i in range...  13.4 us
    ppermute x4, waiting for transfers between devices, on_device(): lax.ppermute(packed[o], 'elem', [((i + offset) % parts, i) for i in range...  7.42 us
    pallas_call x1, Pallas kernels, on_device(): call(planes_kernel, shape((modes, 3, rows, width), BF16), 'planes', scrat...  7.13 us
    all_to_all x1, starting transfers between devices, on_device(): lax.all_to_all(returned, 'mode', split_axis=0, concat_axis=0, tiled=True)  4.25 us
    pallas_call x1, Pallas kernels, on_device(): call(trace_kernel, (shape((8, 2 * rows, slots), BF16), shape((4, 9, NEAR,...  3.66 us
    unnamed x26, local copies, waits for them, and re-layouts  3.53 us
    pallas_call x1, Pallas kernels, on_device(): call(lambda *refs: penalty_kernel(weights, *refs), shape((2, rows, column...  2.89 us
  transfers between devices with their start and end apart: 5, of which 2 were waited for; matrix products, arithmetic and copies ran while one was open for 0% of the time, Pallas kernels for 9%

commit v1 on v0

--- a/solution.py
+++ b/solution.py
@@ -88,67 +88,52 @@
     return rate * jnp.where((row & 1) == 0, above, -below)
 
 
-def planes_kernel(
-    coeff_ref, adv_ref, visc_ref, syn_ref, fwd_ref, bwd_ref, mass_ref, out_ref, stack, back
-):
-    blocks, _, rows, width = coeff_ref.shape
-    total = blocks * rows
-    for b in range(blocks):
-        for f in range(2):
-            values = coeff_ref[b, f]
-            span = pl.ds(b * rows, rows)
-            stack[span, pl.ds(2 * f * width, width)] = values
-            stack[span, pl.ds((2 * f + 1) * width, width)] = span_slope(
-                values.astype(F32), b * rows, total
-            ).astype(BF16)
+def field_planes(field, adv_ref, visc_ref, syn_ref, fwd_ref, bwd_ref, mass_ref, stack, back, out_ref):
+    modes, _, rows, width = out_ref.shape
+    total = modes * rows
+    for b in range(modes):
+        span = pl.ds(b * rows, rows)
+        stack[field, span, pl.ds(width, width)] = span_slope(
+            stack[field, span, pl.ds(0, width)].astype(F32), b * rows, total
+        ).astype(BF16)
     chunk = 256
+    lead = 1 if field == 0 else 0
     for c in range(total // chunk):
         span = pl.ds(c * chunk, chunk)
-        phys = jnp.dot(syn_ref[span, :], stack[...], preferred_element_type=F32)
+        phys = jnp.dot(syn_ref[span, :], stack[field], preferred_element_type=F32)
         weighted = mass_ref[...] * visc_ref[span, :].astype(F32)
-        for f in range(2):
-            plain = phys[:, 2 * f * width : (2 * f + 1) * width]
-            along = phys[:, (2 * f + 1) * width : (2 * f + 2) * width]
-            grads = split_dot(plain, fwd_ref[...])
-            grad_x = grads[:, :width]
-            grad_y = grads[:, width:]
-            if f == 0:
-                moved = (
-                    adv_ref[0, span, :].astype(F32) * grad_x
-                    + adv_ref[1, span, :].astype(F32) * grad_y
-                    + adv_ref[2, span, :].astype(F32) * along
-                )
-                back[span, pl.ds(0, width)] = moved.astype(BF16)
-            flat = split_dot(
-                jnp.concatenate([weighted * grad_x, weighted * grad_y], axis=1), bwd_ref[...]
+        along = phys[:, width:]
+        grads = split_dot(phys[:, :width], fwd_ref[...])
+        grad_x = grads[:, :width]
+        grad_y = grads[:, width:]
+        if field == 0:
+            moved = (
+                adv_ref[0, span, :].astype(F32) * grad_x
+                + adv_ref[1, span, :].astype(F32) * grad_y
+                + adv_ref[2, span, :].astype(F32) * along
             )
-            back[span, pl.ds((2 * f + 1) * width, width)] = flat.astype(BF16)
-            back[span, pl.ds((2 * f + 2) * width, width)] = (weighted * along).astype(BF16)
+            back[span, pl.ds(2 * width, width)] = moved.astype(BF16)
+        flat = split_dot(
+            jnp.concatenate([weighted * grad_x, weighted * grad_y], axis=1), bwd_ref[...]
+        )
+        back[span, pl.ds(0, width)] = flat.astype(BF16)
+        back[span, pl.ds(width, width)] = (weighted * along).astype(BF16)
     for c in range(total // chunk):
         spec = lax.dot_general(
             syn_ref[:, pl.ds(c * chunk, chunk)],
-            back[...],
+            back[:, pl.ds(0, (2 + lead) * width)],
             (((0,), (0,)), ((), ())),
             preferred_element_type=F32,
         )
-        for f in range(3):
-            part = spec[:, :width]
-            if f > 0:
-                low = (2 * f - 1) * width
-                part = spec[:, low : low + width] - span_slope(
-                    spec[:, low + width : low + 2 * width], c * chunk, total
-                )
+        parts = [
+            spec[:, :width] - span_slope(spec[:, width : 2 * width], c * chunk, total)
+        ]
+        if field == 0:
+            parts.append(spec[:, 2 * width :])
+        for i, part in enumerate(parts):
             part = part.astype(BF16)
             for b in range(chunk // rows):
-                out_ref[c * (chunk // rows) + b, f] = part[b * rows : (b + 1) * rows]
-
-
-def split_kernel(u_ref, d_ref, out_ref):
-    width = out_ref.shape[3]
-    for b in range(out_ref.shape[0]):
-        span = pl.ds(b * width, width)
-        out_ref[b, 0] = u_ref[:, span]
-        out_ref[b, 1] = d_ref[:, span]
+                out_ref[c * (chunk // rows) + b, i] = part[b * rows : (b + 1) * rows]
 
 
 class SlotTables:
@@ -197,8 +182,7 @@
         return jnp.where((self.peer_row == peer) & (place == order), 1.0, 0.0)
 
 
-def trace_kernel(u_ref, d_ref, deg_ref, side_ref, link_ref, trace_ref, packed_ref):
-    tables = SlotTables(deg_ref, side_ref, link_ref)
+def send_traces(tables, u_ref, d_ref, left, packed_ref):
     columns = u_ref.shape[1]
     values = jnp.concatenate([u_ref[...], d_ref[...]], axis=0)
     before = tables.sub < tables.lane
@@ -212,7 +196,7 @@
         wanted = (first_col + step_col * float(k)).astype(jnp.int32)
         hot = jnp.where(ids == wanted, 1.0, 0.0).astype(BF16)
         trace = lax.dot_general(values, hot, nt, preferred_element_type=F32).astype(BF16)
-        trace_ref[k] = trace
+        left[pl.ds(0, LANES), pl.ds(k * 2 * LANES, LANES)] = trace
         packed = lax.dot_general(picks_all, trace, nt, preferred_element_type=F32)
         for o in range(4):
             packed_ref[o, k] = packed[o * NEAR : (o + 1) * NEAR].astype(BF16)
@@ -221,24 +205,7 @@
         packed_ref[o, 8] = jnp.broadcast_to(degree, (NEAR, LANES)).astype(BF16)
 
 
-def penalty_kernel(
-    edge_weight,
-    u_ref,
-    d_ref,
-    deg_ref,
-    side_ref,
-    link_ref,
-    mass_ref,
-    trace_ref,
-    near0,
-    near1,
-    near2,
-    near3,
-    out_ref,
-    left,
-):
-    nears = (near0, near1, near2, near3)
-    tables = SlotTables(deg_ref, side_ref, link_ref)
+def local_terms(edge_weight, tables, u_ref, d_ref, mass_ref, nears, left, vel_ref, dir_ref):
     rows, columns = u_ref.shape
     slot_col = tables.column(tables.slot_row)
 
@@ -261,7 +228,7 @@
     for o, offset in enumerate(OFFSETS):
         match = tables.chosen(offset, before)
         flips.append(jnp.sum(match * tables.flip_row, axis=1, keepdims=True))
-        sets.append(aims(match, nears[o][8].astype(F32)[:, 0:1]))
+        sets.append(aims(match, nears[o, 8].astype(F32)[:, 0:1]))
     filler = 2 * LANES - tables.slots - 4 * NEAR
     zeros = jnp.zeros((filler, 1), F32)
 
@@ -278,9 +245,9 @@
     strength = alive * PENALTY * (degree + 1.0) * (degree + 1.0)
     for k in range(8):
         received = jnp.concatenate(
-            [near[k].astype(F32) for near in nears] + [jnp.zeros((filler, LANES), F32)], axis=0
-        )
-        left[pl.ds(0, LANES), pl.ds(k * 2 * LANES, LANES)] = trace_ref[k]
+            [nears[o, k].astype(F32) for o in range(4)] + [jnp.zeros((filler, LANES), F32)],
+            axis=0,
+        )
         left[pl.ds(0, LANES), pl.ds((k * 2 + 1) * LANES, LANES)] = received.T.astype(BF16)
     left[pl.ds(LANES, 16), :] = jnp.ones((16, left.shape[1]), BF16)
     wide = 256
@@ -299,77 +266,211 @@
         summed = jnp.dot(left[...], hot, preferred_element_type=F32)
         scale = mass + summed[LANES : LANES + 1, :]
         span = pl.ds(c * wide, wide)
-        out_ref[0, :, span] = scale * u_ref[:, span].astype(F32) - summed[:rows]
-        out_ref[1, :, span] = scale * d_ref[:, span].astype(F32) - summed[rows : 2 * rows]
-
-
-def final_kernel(back_ref, local_ref, adv_ref, vel_ref, dir_ref):
-    width = back_ref.shape[3]
-    for b in range(back_ref.shape[0]):
+        vel_ref[:, span] = scale * u_ref[:, span].astype(F32) - summed[:rows]
+        dir_ref[:, span] = scale * d_ref[:, span].astype(F32) - summed[rows : 2 * rows]
+
+
+ROUTES = [(dz, dc) for dz in (4, 3, 5, 2, 6, 1, 7, 0) for dc in (0, 1) if (dz, dc) != (0, 0)]
+
+
+def whole_kernel(
+    edge_weight,
+    u_ref,
+    d_ref,
+    adv_hbm,
+    visc_hbm,
+    deg_ref,
+    side_ref,
+    link_ref,
+    syn_hbm,
+    fwd_ref,
+    bwd_ref,
+    mass_ref,
+    adv_out,
+    vel_out,
+    dir_out,
+    adv_ref,
+    visc_ref,
+    syn_ref,
+    stack,
+    back,
+    ret_u,
+    ret_d,
+    got_u,
+    got_d,
+    left,
+    packed,
+    nears,
+    load_sem,
+    in_send,
+    in_recv,
+    u_send,
+    u_recv,
+    d_send,
+    d_recv,
+    halo_send,
+    halo_recv,
+):
+    elem = lax.axis_index("elem")
+    mode = lax.axis_index("mode")
+    parts = lax.axis_size("elem")
+    chips = lax.axis_size("mode") // 2
+    chip = lax.div(mode, 2)
+    core = lax.rem(mode, 2)
+    rows = u_ref.shape[0]
+    width = visc_ref.shape[1]
+    modes_to = [
+        lax.rem(chip + dz, chips) * 2 + lax.rem(core + dc, 2) for dz, dc in ROUTES
+    ]
+    elems_to = [lax.rem(elem + offset + parts, parts) for offset in OFFSETS]
+    mesh_ids = pl.DeviceIdType.MESH
+
+    barrier = pltpu.get_barrier_semaphore()
+    for other in modes_to:
+        pl.semaphore_signal(barrier, inc=1, device_id=(elem, other), device_id_type=mesh_ids)
+    for other in elems_to:
+        pl.semaphore_signal(barrier, inc=1, device_id=(other, mode), device_id_type=mesh_ids)
+    loads = [
+        pltpu.make_async_copy(syn_hbm, syn_ref, load_sem.at[0]),
+        pltpu.make_async_copy(visc_hbm, visc_ref, load_sem.at[1]),
+        pltpu.make_async_copy(adv_hbm, adv_ref, load_sem.at[2]),
+    ]
+    for load in loads:
+        load.start()
+    pl.semaphore_wait(barrier, len(modes_to) + len(elems_to))
+
+    my_rows = pl.ds(pl.multiple_of(mode * rows, rows), rows)
+    incoming = []
+    for f, source in enumerate((u_ref, d_ref)):
+        copies = []
+        for j, other in enumerate(modes_to):
+            copy = pltpu.make_async_remote_copy(
+                src_ref=source.at[:, pl.ds(pl.multiple_of(other * width, width), width)],
+                dst_ref=stack.at[f, my_rows, pl.ds(0, width)],
+                send_sem=in_send.at[f, j],
+                recv_sem=in_recv.at[f, j],
+                device_id=(elem, other),
+                device_id_type=mesh_ids,
+            )
+            copy.start()
+            copies.append(copy)
+        incoming.append(copies)
+    tables = SlotTables(deg_ref, side_ref, link_ref)
+    send_traces(tables, u_ref, d_ref, left, packed)
+    halo = []
+    for o, other in enumerate(elems_to):
+        copy = pltpu.make_async_remote_copy(
+            src_ref=packed.at[o],
+            dst_ref=nears.at[(o + 2) % 4],
+            send_sem=halo_send.at[o],
+            recv_sem=halo_recv.at[o],
+            device_id=(other, mode),
+            device_id_type=mesh_ids,
+        )
+        copy.start()
+        halo.append(copy)
+    for f, source in enumerate((u_ref, d_ref)):
+        stack[f, my_rows, pl.ds(0, width)] = source[
+            :, pl.ds(pl.multiple_of(mode * width, width), width)
+        ]
+    for load in loads:
+        load.wait()
+    outgoing = []
+    for f, (ret, got, send, recv) in enumerate(
+        ((ret_u, got_u, u_send, u_recv), (ret_d, got_d, d_send, d_recv))
+    ):
+        for copy in incoming[f]:
+            copy.wait_recv()
+        field_planes(
+            f, adv_ref, visc_ref, syn_ref, fwd_ref, bwd_ref, mass_ref, stack, back, ret
+        )
+        copies = []
+        for j, other in enumerate(modes_to):
+            copy = pltpu.make_async_remote_copy(
+                src_ref=ret.at[other],
+                dst_ref=got.at[mode],
+                send_sem=send.at[j],
+                recv_sem=recv.at[j],
+                device_id=(elem, other),
+                device_id_type=mesh_ids,
+            )
+            copy.start()
+            copies.append(copy)
+        got[mode] = ret[mode]
+        outgoing.append(copies)
+    for copy in halo:
+        copy.wait_recv()
+    local_terms(edge_weight, tables, u_ref, d_ref, mass_ref, nears, left, vel_out, dir_out)
+    for copy in outgoing[0]:
+        copy.wait_recv()
+    for b in range(got_u.shape[0]):
         span = pl.ds(b * width, width)
-        adv_ref[:, span] = back_ref[b, 0].astype(F32)
-        vel_ref[:, span] = local_ref[0, :, span] + back_ref[b, 1].astype(F32)
-        dir_ref[:, span] = local_ref[1, :, span] + back_ref[b, 2].astype(F32)
-
-
-def call(kernel, outs, name, scratch=(), cost=None):
-    return pl.pallas_call(
-        kernel,
-        out_shape=outs,
-        scratch_shapes=list(scratch),
-        name=name,
-        cost_estimate=cost,
-        compiler_params=pltpu.CompilerParams(vmem_limit_bytes=48 * 1024 * 1024),
-    )
-
-
-def cost(flops, moved):
-    return pl.CostEstimate(flops=flops, bytes_accessed=moved, transcendentals=0)
+        vel_out[:, span] += got_u[b, 0].astype(F32)
+        adv_out[:, span] = got_u[b, 1].astype(F32)
+    for copy in outgoing[1]:
+        copy.wait_recv()
+    for b in range(got_d.shape[0]):
+        span = pl.ds(b * width, width)
+        dir_out[:, span] += got_d[b, 0].astype(F32)
+    for copy in incoming[0] + incoming[1] + halo + outgoing[0] + outgoing[1]:
+        copy.wait_send()
 
 
 def on_device(u_spec, dir_spec, advecting, viscosity, degrees, edge_side, edge_link):
-    shape = jax.ShapeDtypeStruct
     modes = lax.axis_size("mode")
     total, width = viscosity.shape
     rows, columns = u_spec.shape
     forward, backward, mass = operator_tables(degrees.shape[1] // modes)
     weights = LENGTH * cheb_tables()[1]
-    side = edge_side[None, :]
-    slots = edge_side.shape[0]
-
-    sent = call(split_kernel, shape((modes, 2, rows, width), BF16), "split")(u_spec, dir_spec)
-    coeffs = lax.all_to_all(sent, "mode", split_axis=0, concat_axis=0, tiled=True)
-
-    traces, packed = call(
-        trace_kernel,
-        (shape((8, 2 * rows, slots), BF16), shape((4, 9, NEAR, LANES), BF16)),
-        "trace",
-        cost=cost(1 << 29, 1 << 20),
-    )(u_spec, dir_spec, degrees, side, edge_link)
-    parts = lax.axis_size("elem")
-    nears = [
-        lax.ppermute(packed[o], "elem", [((i + offset) % parts, i) for i in range(parts)])
-        for o, offset in enumerate((-d for d in OFFSETS))
-    ]
-    nears = [nears[2], nears[3], nears[0], nears[1]]
-    local = call(
-        lambda *refs: penalty_kernel(weights, *refs),
-        shape((2, rows, columns), F32),
-        "penalty",
-        scratch=[pltpu.VMEM((LANES + 16, 16 * LANES), BF16)],
-        cost=cost(1 << 30, 1 << 21),
-    )(u_spec, dir_spec, degrees, side, edge_link, mass, traces, *nears)
-
-    returned = call(
-        planes_kernel,
-        shape((modes, 3, rows, width), BF16),
-        "planes",
-        scratch=[pltpu.VMEM((total, 4 * width), BF16), pltpu.VMEM((total, 5 * width), BF16)],
-        cost=cost(1 << 32, 1 << 22),
-    )(coeffs, advecting, viscosity, synthesis_table(total), forward, backward, mass)
-    volumes = lax.all_to_all(returned, "mode", split_axis=0, concat_axis=0, tiled=True)
-    out = shape((rows, columns), F32)
-    return call(final_kernel, (out, out, out), "final")(volumes, local)
+    out = jax.ShapeDtypeStruct((rows, columns), F32)
+    near = pl.BlockSpec(memory_space=pltpu.VMEM)
+    far = pl.BlockSpec(memory_space=pltpu.HBM)
+    routes = len(ROUTES)
+    return pl.pallas_call(
+        lambda *refs: whole_kernel(weights, *refs),
+        out_shape=(out, out, out),
+        in_specs=[near, near, far, far, near, near, near, far, near, near, near],
+        out_specs=(near, near, near),
+        scratch_shapes=[
+            pltpu.VMEM((3, total, width), BF16),
+            pltpu.VMEM((total, width), BF16),
+            pltpu.VMEM((total, total), BF16),
+            pltpu.VMEM((2, total, 2 * width), BF16),
+            pltpu.VMEM((total, 3 * width), BF16),
+            pltpu.VMEM((modes, 2, rows, width), BF16),
+            pltpu.VMEM((modes, 1, rows, width), BF16),
+            pltpu.VMEM((modes, 2, rows, width), BF16),
+            pltpu.VMEM((modes, 1, rows, width), BF16),
+            pltpu.VMEM((LANES + 16, 16 * LANES), BF16),
+            pltpu.VMEM((4, 9, NEAR, LANES), BF16),
+            pltpu.VMEM((4, 9, NEAR, LANES), BF16),
+            pltpu.SemaphoreType.DMA((3,)),
+            pltpu.SemaphoreType.DMA((2, routes)),
+            pltpu.SemaphoreType.DMA((2, routes)),
+            pltpu.SemaphoreType.DMA((routes,)),
+            pltpu.SemaphoreType.DMA((routes,)),
+            pltpu.SemaphoreType.DMA((routes,)),
+            pltpu.SemaphoreType.DMA((routes,)),
+            pltpu.SemaphoreType.DMA((4,)),
+            pltpu.SemaphoreType.DMA((4,)),
+        ],
+        name="whole",
+        compiler_params=pltpu.CompilerParams(
+            collective_id=0, has_side_effects=True, vmem_limit_bytes=48 * 1024 * 1024
+        ),
+    )(
+        u_spec,
+        dir_spec,
+        advecting,
+        viscosity,
+        degrees,
+        edge_side[None, :],
+        edge_link,
+        synthesis_table(total),
+        forward,
+        backward,
+        mass,
+    )
 
 
 def solution(mesh):

time: 71.2 us -> 61.3 us (0.86)
  the two profiles are of different devices: /device:TPU:30 before, /device:TPU:1 now
where the time goes in v1:
time: 61.3 us; the launch traced here: 60.9 us
  Pallas kernels  47.7 us (78%)
  local copies, waits for them, and re-layouts  12.5 us (20%)
  between operations  0.66 us (1%)
    pallas_call x1, Pallas kernels, on_device(): pl.pallas_call(lambda *refs: whole_kernel(weights, *refs), out_shape=(out...  47.7 us
    unnamed x25, local copies, waits for them, and re-layouts  12.5 us

profile of v1, /device:TPU:1, one launch (start us, length us, event | category | flops | bytes accessed | tf_op | source)
XLA Modules:
  0.0 60.9 jit_solution(13147098113825184566)
XLA Ops:
  0.6 0.0 copy-start
  0.6 1.6 %copy-done = bf16[1024,1024]{1,0:T(8,128)(2,1)S(1)} copy-done((bf16[1024,1024]{1,0:T(8,128)(2,1)S(1)}, bf16[1024,1024]{1,0:T(8,128)(2,1)}, u32[]{:S(2)}) %copy-start) | copy-done | bytes 2097176
  2.2 0.0 copy-start.1
  2.2 1.1 %copy-done.1 = bf16[3,1024,128]{2,1,0:T(8,128)(2,1)S(1)} copy-done((bf16[3,1024,128]{2,1,0:T(8,128)(2,1)S(1)}, bf16[3,1024,128]{2,1,0:T(8,128)(2,1)}, u32[]{:S(2)}) %copy-start.1) | copy-done | bytes 786456
  3.4 0.0 copy-start.2
  3.4 0.9 %copy-done.2 = bf16[64,2048]{1,0:T(8,128)(2,1)S(1)} copy-done((bf16[64,2048]{1,0:T(8,128)(2,1)S(1)}, bf16[64,2048]{1,0:T(8,128)(2,1)}, u32[]{:S(2)}) %copy-start.2) | copy-done | bytes 262168
  4.3 0.0 copy-start.3
  4.3 0.9 %copy-done.3 = bf16[64,2048]{1,0:T(8,128)(2,1)S(1)} copy-done((bf16[64,2048]{1,0:T(8,128)(2,1)S(1)}, bf16[64,2048]{1,0:T(8,128)(2,1)}, u32[]{:S(2)}) %copy-start.3) | copy-done | bytes 262168
  5.3 0.0 copy-start.4
  5.3 0.9 %copy-done.4 = bf16[1024,128]{1,0:T(8,128)(2,1)S(1)} copy-done((bf16[1024,128]{1,0:T(8,128)(2,1)S(1)}, bf16[1024,128]{1,0:T(8,128)(2,1)}, u32[]{:S(2)}) %copy-start.4) | copy-done | bytes 262168
  6.2 0.0 copy-start.5
  6.2 0.9 %copy-done.5 = bf16[768,128]{1,0:T(8,128)(2,1)S(1)} copy-done((bf16[768,128]{1,0:T(8,128)(2,1)S(1)}, bf16[768,128]{1,0:T(8,128)(2,1)}, u32[]{:S(2)}) %copy-start.5) | copy-done | bytes 196632
  7.1 0.0 copy-start.6
  7.1 0.9 %copy-done.6 = bf16[384,256]{1,0:T(8,128)(2,1)S(1)} copy-done((bf16[384,256]{1,0:T(8,128)(2,1)S(1)}, bf16[384,256]{1,0:T(8,128)(2,1)}, u32[]{:S(2)}) %copy-start.6) | copy-done | bytes 196632
  8.1 0.0 copy-start.7
  8.1 0.7 %copy-done.7 = s32[3,128]{1,0:T(4,128)S(1)} copy-done((s32[3,128]{1,0:T(4,128)S(1)}, s32[3,128]{1,0:T(4,128)}, u32[]{:S(2)}) %copy-start.7) | copy-done | bytes 1560
  8.7 0.0 copy-start.8
  8.8 0.7 %copy-done.8 = s32[2,32]{1,0:T(2,128)S(1)} copy-done((s32[2,32]{1,0:T(2,128)S(1)}, s32[2,32]{1,0:T(2,128)}, u32[]{:S(2)}) %copy-start.8) | copy-done | bytes 280
  9.4 0.0 copy-start.9
  9.4 0.7 %copy-done.9 = s32[128]{0:T(128)S(1)} copy-done((s32[128]{0:T(128)S(1)}, s32[128]{0:T(128)}, u32[]{:S(2)}) %copy-start.9) | copy-done | bytes 536
  10.1 0.0 copy-start.10
  10.1 0.7 %copy-done.10 = f32[1,128]{1,0:T(1,128)S(1)} copy-done((f32[1,128]{1,0:T(1,128)S(1)}, f32[1,128]{1,0:T(1,128)}, u32[]{:S(2)}) %copy-start.10) | copy-done | bytes 536
  10.7 47.7 %whole.1 = (f32[64,2048]{1,0:T(8,128)S(1)}, f32[64,2048]{1,0:T(8,128)S(1)}, f32[64,2048]{1,0:T(8,128)S(1)}) custom-call(bf16[64,2048]{1,0:T(8,128)(2,1)S(1)} %copy-done.2, bf16[64,2048]{1,0:T(8,128)(2,1)S(1)} %copy-done.3, bf16[3,1024,128]{2,1,0:T(8,128)(2,1)S(1)} %copy-done.1, bf16[1024,128]{1,0:T(8,128)(2,1)S(1)} %copy-done.4, s32[2,32]{1,0:T(2,128)S(1)} %copy-done.8, ...), custom_call_target="tpu_custom_call" | custom-call | tf_op jit(solution)/shard_map/whole/pallas_call | solution.py:429
  58.5 0.8 %copy.17 = f32[64,2048]{1,0:T(8,128)} copy(f32[64,2048]{1,0:T(8,128)S(1)} %get-tuple-element.6) | data formatting | bytes 1048576
  59.3 0.8 %copy.18 = f32[64,2048]{1,0:T(8,128)} copy(f32[64,2048]{1,0:T(8,128)S(1)} %get-tuple-element.7) | data formatting | bytes 1048576
  60.1 0.8 %copy.19 = f32[64,2048]{1,0:T(8,128)} copy(f32[64,2048]{1,0:T(8,128)S(1)} %get-tuple-element.8) | data formatting | bytes 1048576
Async XLA Ops:
  0.6 1.6 %copy-start = (bf16[1024,1024]{1,0:T(8,128)(2,1)S(1)}, bf16[1024,1024]{1,0:T(8,128)(2,1)}, u32[]{:S(2)}) copy-start(bf16[1024,1024]{1,0:T(8,128)(2,1)} %constant.8.clone.refs_7_) | copy-start | bytes 6291460
  2.2 1.1 %copy-start.1 = (bf16[3,1024,128]{2,1,0:T(8,128)(2,1)S(1)}, bf16[3,1024,128]{2,1,0:T(8,128)(2,1)}, u32[]{:S(2)}) copy-start(bf16[3,1024,128]{2,1,0:T(8,128)(2,1)} %refs_2_.1) | copy-start | bytes 2359300
  3.4 0.9 %copy-start.2 = (bf16[64,2048]{1,0:T(8,128)(2,1)S(1)}, bf16[64,2048]{1,0:T(8,128)(2,1)}, u32[]{:S(2)}) copy-start(bf16[64,2048]{1,0:T(8,128)(2,1)} %refs_0_.1) | copy-start | bytes 786436
  4.3 0.9 %copy-start.3 = (bf16[64,2048]{1,0:T(8,128)(2,1)S(1)}, bf16[64,2048]{1,0:T(8,128)(2,1)}, u32[]{:S(2)}) copy-start(bf16[64,2048]{1,0:T(8,128)(2,1)} %refs_1_.1) | copy-start | bytes 786436
  5.3 0.9 %copy-start.4 = (bf16[1024,128]{1,0:T(8,128)(2,1)S(1)}, bf16[1024,128]{1,0:T(8,128)(2,1)}, u32[]{:S(2)}) copy-start(bf16[1024,128]{1,0:T(8,128)(2,1)} %refs_3_.1) | copy-start | bytes 786436
  6.2 0.9 %copy-start.5 = (bf16[768,128]{1,0:T(8,128)(2,1)S(1)}, bf16[768,128]{1,0:T(8,128)(2,1)}, u32[]{:S(2)}) copy-start(bf16[768,128]{1,0:T(8,128)(2,1)} %constant.10.clone.refs_9_) | copy-start | bytes 589828
  7.1 0.9 %copy-start.6 = (bf16[384,256]{1,0:T(8,128)(2,1)S(1)}, bf16[384,256]{1,0:T(8,128)(2,1)}, u32[]{:S(2)}) copy-start(bf16[384,256]{1,0:T(8,128)(2,1)} %constant.9.clone.refs_8_) | copy-start | bytes 589828
  8.1 0.7 %copy-start.7 = (s32[3,128]{1,0:T(4,128)S(1)}, s32[3,128]{1,0:T(4,128)}, u32[]{:S(2)}) copy-start(s32[3,128]{1,0:T(4,128)} %refs_6_.1) | copy-start | bytes 4612
  8.7 0.7 %copy-start.8 = (s32[2,32]{1,0:T(2,128)S(1)}, s32[2,32]{1,0:T(2,128)}, u32[]{:S(2)}) copy-start(s32[2,32]{1,0:T(2,128)} %refs_4_.1) | copy-start | bytes 772
  9.4 0.7 %copy-start.9 = (s32[128]{0:T(128)S(1)}, s32[128]{0:T(128)}, u32[]{:S(2)}) copy-start(s32[128]{0:T(128)} %param.16) | copy-start | bytes 1540
  10.1 0.7 %copy-start.10 = (f32[1,128]{1,0:T(1,128)S(1)}, f32[1,128]{1,0:T(1,128)}, u32[]{:S(2)}) copy-start(f32[1,128]{1,0:T(1,128)} %constant.11.clone.refs_10_) | copy-start | bytes 1540

commit v2 on v1

--- a/solution.py
+++ b/solution.py
@@ -275,29 +275,33 @@
 
 def whole_kernel(
     edge_weight,
-    u_ref,
-    d_ref,
+    u_hbm,
+    d_hbm,
     adv_hbm,
     visc_hbm,
+    syn_hbm,
+    fwd_hbm,
+    bwd_hbm,
+    mass_hbm,
     deg_ref,
     side_ref,
     link_ref,
-    syn_hbm,
+    got_u,
+    got_d,
+    local_hbm,
+    u_ref,
+    d_ref,
+    adv_ref,
+    visc_ref,
+    syn_ref,
     fwd_ref,
     bwd_ref,
     mass_ref,
-    adv_out,
-    vel_out,
-    dir_out,
-    adv_ref,
-    visc_ref,
-    syn_ref,
+    local,
     stack,
     back,
     ret_u,
     ret_d,
-    got_u,
-    got_d,
     left,
     packed,
     nears,
@@ -330,10 +334,19 @@
         pl.semaphore_signal(barrier, inc=1, device_id=(elem, other), device_id_type=mesh_ids)
     for other in elems_to:
         pl.semaphore_signal(barrier, inc=1, device_id=(other, mode), device_id_type=mesh_ids)
+    pairs = (
+        (u_hbm, u_ref),
+        (d_hbm, d_ref),
+        (syn_hbm, syn_ref),
+        (fwd_hbm, fwd_ref),
+        (bwd_hbm, bwd_ref),
+        (mass_hbm, mass_ref),
+        (visc_hbm, visc_ref),
+        (adv_hbm, adv_ref),
+    )
     loads = [
-        pltpu.make_async_copy(syn_hbm, syn_ref, load_sem.at[0]),
-        pltpu.make_async_copy(visc_hbm, visc_ref, load_sem.at[1]),
-        pltpu.make_async_copy(adv_hbm, adv_ref, load_sem.at[2]),
+        pltpu.make_async_copy(source, target, load_sem.at[i])
+        for i, (source, target) in enumerate(pairs)
     ]
     for load in loads:
         load.start()
@@ -341,7 +354,7 @@
 
     my_rows = pl.ds(pl.multiple_of(mode * rows, rows), rows)
     incoming = []
-    for f, source in enumerate((u_ref, d_ref)):
+    for f, source in enumerate((u_hbm, d_hbm)):
         copies = []
         for j, other in enumerate(modes_to):
             copy = pltpu.make_async_remote_copy(
@@ -356,6 +369,8 @@
             copies.append(copy)
         incoming.append(copies)
     tables = SlotTables(deg_ref, side_ref, link_ref)
+    for load in loads[:2]:
+        load.wait()
     send_traces(tables, u_ref, d_ref, left, packed)
     halo = []
     for o, other in enumerate(elems_to):
@@ -373,9 +388,10 @@
         stack[f, my_rows, pl.ds(0, width)] = source[
             :, pl.ds(pl.multiple_of(mode * width, width), width)
         ]
-    for load in loads:
+    for load in loads[2:]:
         load.wait()
     outgoing = []
+    stores = []
     for f, (ret, got, send, recv) in enumerate(
         ((ret_u, got_u, u_send, u_recv), (ret_d, got_d, d_send, d_recv))
     ):
@@ -396,24 +412,36 @@
             )
             copy.start()
             copies.append(copy)
-        got[mode] = ret[mode]
+        store = pltpu.make_async_copy(ret.at[mode], got.at[mode], load_sem.at[8 + f])
+        store.start()
+        stores.append(store)
         outgoing.append(copies)
     for copy in halo:
         copy.wait_recv()
-    local_terms(edge_weight, tables, u_ref, d_ref, mass_ref, nears, left, vel_out, dir_out)
-    for copy in outgoing[0]:
+    local_terms(
+        edge_weight, tables, u_ref, d_ref, mass_ref, nears, left, local.at[0], local.at[1]
+    )
+    store = pltpu.make_async_copy(local, local_hbm, load_sem.at[10])
+    store.start()
+    stores.append(store)
+    for copy in outgoing[0] + outgoing[1]:
         copy.wait_recv()
+    for store in stores:
+        store.wait()
+    for copy in incoming[0] + incoming[1] + halo + outgoing[0] + outgoing[1]:
+        copy.wait_send()
+
+
+def final_kernel(got_u, got_d, local, adv_out, vel_out, dir_out):
+    width = got_u.shape[3]
     for b in range(got_u.shape[0]):
         span = pl.ds(b * width, width)
-        vel_out[:, span] += got_u[b, 0].astype(F32)
+        vel_out[:, span] = local[0, :, span] + got_u[b, 0].astype(F32)
         adv_out[:, span] = got_u[b, 1].astype(F32)
-    for copy in outgoing[1]:
-        copy.wait_recv()
-    for b in range(got_d.shape[0]):
-        span = pl.ds(b * width, width)
-        dir_out[:, span] += got_d[b, 0].astype(F32)
-    for copy in incoming[0] + incoming[1] + halo + outgoing[0] + outgoing[1]:
-        copy.wait_send()
+        dir_out[:, span] = local[1, :, span] + got_d[b, 0].astype(F32)
+
+
+VMEM_BYTES = 67043328
 
 
 def on_device(u_spec, dir_spec, advecting, viscosity, degrees, edge_side, edge_link):
@@ -422,29 +450,37 @@
     rows, columns = u_spec.shape
     forward, backward, mass = operator_tables(degrees.shape[1] // modes)
     weights = LENGTH * cheb_tables()[1]
-    out = jax.ShapeDtypeStruct((rows, columns), F32)
+    shape = jax.ShapeDtypeStruct
     near = pl.BlockSpec(memory_space=pltpu.VMEM)
     far = pl.BlockSpec(memory_space=pltpu.HBM)
     routes = len(ROUTES)
-    return pl.pallas_call(
+    got_u, got_d, local = pl.pallas_call(
         lambda *refs: whole_kernel(weights, *refs),
-        out_shape=(out, out, out),
-        in_specs=[near, near, far, far, near, near, near, far, near, near, near],
-        out_specs=(near, near, near),
+        out_shape=(
+            shape((modes, 2, rows, width), BF16),
+            shape((modes, 1, rows, width), BF16),
+            shape((2, rows, columns), F32),
+        ),
+        in_specs=[far] * 8 + [near] * 3,
+        out_specs=(far, far, far),
         scratch_shapes=[
+            pltpu.VMEM((rows, columns), BF16),
+            pltpu.VMEM((rows, columns), BF16),
             pltpu.VMEM((3, total, width), BF16),
             pltpu.VMEM((total, width), BF16),
             pltpu.VMEM((total, total), BF16),
+            pltpu.VMEM(forward.shape, BF16),
+            pltpu.VMEM(backward.shape, BF16),
+            pltpu.VMEM(mass.shape, F32),
+            pltpu.VMEM((2, rows, columns), F32),
             pltpu.VMEM((2, total, 2 * width), BF16),
             pltpu.VMEM((total, 3 * width), BF16),
-            pltpu.VMEM((modes, 2, rows, width), BF16),
-            pltpu.VMEM((modes, 1, rows, width), BF16),
             pltpu.VMEM((modes, 2, rows, width), BF16),
             pltpu.VMEM((modes, 1, rows, width), BF16),
             pltpu.VMEM((LANES + 16, 16 * LANES), BF16),
             pltpu.VMEM((4, 9, NEAR, LANES), BF16),
             pltpu.VMEM((4, 9, NEAR, LANES), BF16),
-            pltpu.SemaphoreType.DMA((3,)),
+            pltpu.SemaphoreType.DMA((11,)),
             pltpu.SemaphoreType.DMA((2, routes)),
             pltpu.SemaphoreType.DMA((2, routes)),
             pltpu.SemaphoreType.DMA((routes,)),
@@ -456,21 +492,28 @@
         ],
         name="whole",
         compiler_params=pltpu.CompilerParams(
-            collective_id=0, has_side_effects=True, vmem_limit_bytes=48 * 1024 * 1024
+            collective_id=0, has_side_effects=True, vmem_limit_bytes=VMEM_BYTES
         ),
     )(
         u_spec,
         dir_spec,
         advecting,
         viscosity,
-        degrees,
-        edge_side[None, :],
-        edge_link,
         synthesis_table(total),
         forward,
         backward,
         mass,
-    )
+        degrees,
+        edge_side[None, :],
+        edge_link,
+    )
+    out = shape((rows, columns), F32)
+    return pl.pallas_call(
+        final_kernel,
+        out_shape=(out, out, out),
+        name="final",
+        compiler_params=pltpu.CompilerParams(vmem_limit_bytes=VMEM_BYTES),
+    )(got_u, got_d, local)
 
 
 def solution(mesh):

time: 61.3 us -> 52.3 us (0.85)
  local copies, waits for them, and re-layouts: 12.5 us -> 0 us
  Pallas kernels: 47.7 us -> 51.5 us
    unnamed x25 -> x0, local copies, waits for them, and re-layouts: 12.5 us -> none
    pallas_call x1 -> x2, Pallas kernels: 47.7 us -> 51.5 us  [the longest x1 48.8 us: on_device(): pl.pallas_call(lambda *refs: whole_kernel(weights, *refs), out_shape=(sha...]
where the time goes in v2:
time: 52.3 us; the launch traced here: 52.1 us
  Pallas kernels  51.5 us (98%)
  between operations  0.64 us (1%)
    pallas_call x1, Pallas kernels, on_device(): pl.pallas_call(lambda *refs: whole_kernel(weights, *refs), out_shape=(sha...  48.8 us
    pallas_call x1, Pallas kernels, on_device(): pl.pallas_call(final_kernel, out_shape=(out, out, out), name='final', com...  2.66 us

profile of v2, /device:TPU:1, one launch (start us, length us, event | category | flops | bytes accessed | tf_op | source)
XLA Modules:
  0.0 52.1 jit_solution(8837134293176122762)
XLA Ops:
  0.6 48.8 %whole.1 = (bf16[16,2,64,128]{3,2,1,0:T(8,128)(2,1)}, bf16[16,1,64,128]{3,2,1,0:T(8,128)(2,1)}, f32[2,64,2048]{2,1,0:T(8,128)}) custom-call(bf16[64,2048]{1,0:T(8,128)(2,1)} %refs_0_.1, bf16[64,2048]{1,0:T(8,128)(2,1)} %refs_1_.1, bf16[3,1024,128]{2,1,0:T(8,128)(2,1)} %refs_2_.1, bf16[1024,128]{1,0:T(8,128)(2,1)} %refs_3_.1, ...), custom_call_target="tpu_custom_call" | custom-call | tf_op jit(solution)/shard_map/whole/pallas_call | solution.py:457
  49.5 2.7 %final.1 = (f32[64,2048]{1,0:T(8,128)}, f32[64,2048]{1,0:T(8,128)}, f32[64,2048]{1,0:T(8,128)}) custom-call(bf16[16,2,64,128]{3,2,1,0:T(8,128)(2,1)} %get-tuple-element.6.got_u, bf16[16,1,64,128]{3,2,1,0:T(8,128)(2,1)} %get-tuple-element.7.got_d, f32[2,64,2048]{2,1,0:T(8,128)} %get-tuple-element.8.local), custom_call_target="tpu_custom_call" | custom-call | tf_op jit(solution)/shard_map/final/pallas_call | solution.py:511

commit v3 on v2

--- a/solution.py
+++ b/solution.py
@@ -314,6 +314,10 @@
     d_recv,
     halo_send,
     halo_recv,
+    relay_in,
+    relay_u,
+    leg_send,
+    leg_recv,
 ):
     elem = lax.axis_index("elem")
     mode = lax.axis_index("mode")
@@ -353,21 +357,65 @@
     pl.semaphore_wait(barrier, len(modes_to) + len(elems_to))
 
     my_rows = pl.ds(pl.multiple_of(mode * rows, rows), rows)
-    incoming = []
-    for f, source in enumerate((u_hbm, d_hbm)):
-        copies = []
-        for j, other in enumerate(modes_to):
-            copy = pltpu.make_async_remote_copy(
-                src_ref=source.at[:, pl.ds(pl.multiple_of(other * width, width), width)],
-                dst_ref=stack.at[f, my_rows, pl.ds(0, width)],
-                send_sem=in_send.at[f, j],
-                recv_sem=in_recv.at[f, j],
-                device_id=(elem, other),
-                device_id_type=mesh_ids,
+    up = lax.rem(chip + 2, chips)
+    down = lax.rem(chip + chips - 2, chips)
+    swapped = lax.rem(core + 1, 2)
+    relays = (up * 2 + core, down * 2 + core)
+    origins = (down * 2 + core, up * 2 + core)
+    onward = (up * 2 + core, down * 2 + swapped)
+
+    def remote(source, target, send, recv, other):
+        copy = pltpu.make_async_remote_copy(
+            src_ref=source,
+            dst_ref=target,
+            send_sem=send,
+            recv_sem=recv,
+            device_id=(elem, other),
+            device_id_type=mesh_ids,
+        )
+        copy.start()
+        return copy
+
+    def block_of(index, size):
+        return pl.ds(pl.multiple_of(index * size, size), size)
+
+    def send_block(f, source, j):
+        other = modes_to[j]
+        return remote(
+            source.at[:, block_of(other, width)],
+            stack.at[f, my_rows, pl.ds(0, width)],
+            in_send.at[f, j],
+            in_recv.at[f, j],
+            other,
+        )
+
+    sources = (u_hbm, d_hbm)
+    legs = [
+        remote(
+            sources[f].at[:, block_of(modes_to[t], width)],
+            relay_in.at[f, t],
+            leg_send.at[f, t],
+            leg_recv.at[f, t],
+            relays[t],
+        )
+        for f in range(2)
+        for t in range(2)
+    ]
+    incoming = [[send_block(0, u_hbm, j) for j in range(2, len(ROUTES))], []]
+    for leg in legs:
+        leg.wait_recv()
+    for f in range(2):
+        for t in range(2):
+            incoming[f].append(
+                remote(
+                    relay_in.at[f, t],
+                    stack.at[f, block_of(origins[t], rows), pl.ds(0, width)],
+                    in_send.at[f, t],
+                    in_recv.at[f, t],
+                    onward[t],
+                )
             )
-            copy.start()
-            copies.append(copy)
-        incoming.append(copies)
+    incoming[1] += [send_block(1, d_hbm, j) for j in range(2, len(ROUTES))]
     tables = SlotTables(deg_ref, side_ref, link_ref)
     for load in loads[:2]:
         load.wait()
@@ -401,17 +449,26 @@
             f, adv_ref, visc_ref, syn_ref, fwd_ref, bwd_ref, mass_ref, stack, back, ret
         )
         copies = []
-        for j, other in enumerate(modes_to):
-            copy = pltpu.make_async_remote_copy(
-                src_ref=ret.at[other],
-                dst_ref=got.at[mode],
-                send_sem=send.at[j],
-                recv_sem=recv.at[j],
-                device_id=(elem, other),
-                device_id_type=mesh_ids,
-            )
-            copy.start()
-            copies.append(copy)
+        if f == 0:
+            legs_u = [
+                remote(
+                    ret.at[modes_to[t]], relay_u.at[t], leg_send.at[2, t], leg_recv.at[2, t],
+                    relays[t],
+                )
+                for t in range(2)
+            ]
+        else:
+            for t in range(2):
+                legs_u[t].wait_recv()
+                outgoing[0].append(
+                    remote(
+                        relay_u.at[t], got_u.at[origins[t]], u_send.at[t], u_recv.at[t],
+                        onward[t],
+                    )
+                )
+        for j in range(2 if f == 0 else 0, len(ROUTES)):
+            other = modes_to[j]
+            copies.append(remote(ret.at[other], got.at[mode], send.at[j], recv.at[j], other))
         store = pltpu.make_async_copy(ret.at[mode], got.at[mode], load_sem.at[8 + f])
         store.start()
         stores.append(store)
@@ -428,7 +485,7 @@
         copy.wait_recv()
     for store in stores:
         store.wait()
-    for copy in incoming[0] + incoming[1] + halo + outgoing[0] + outgoing[1]:
+    for copy in incoming[0] + incoming[1] + halo + outgoing[0] + outgoing[1] + legs + legs_u:
         copy.wait_send()
 
 
@@ -489,6 +546,10 @@
             pltpu.SemaphoreType.DMA((routes,)),
             pltpu.SemaphoreType.DMA((4,)),
             pltpu.SemaphoreType.DMA((4,)),
+            pltpu.VMEM((2, 2, rows, width), BF16),
+            pltpu.VMEM((2, 2, rows, width), BF16),
+            pltpu.SemaphoreType.DMA((3, 2)),
+            pltpu.SemaphoreType.DMA((3, 2)),
         ],
         name="whole",
         compiler_params=pltpu.CompilerParams(

time: 52.3 us -> 53.7 us (1.027)
  Pallas kernels: 51.5 us -> 52.9 us
    pallas_call x1, Pallas kernels: 48.8 us -> 50.2 us  [on_device(): pl.pallas_call(lambda *refs: whole_kernel(weights, *refs), out_shape=(sha...]
where the time goes in v3:
time: 53.7 us; the launch traced here: 53.5 us
  Pallas kernels  52.9 us (99%)
  between operations  0.64 us (1%)
    pallas_call x1, Pallas kernels, on_device(): pl.pallas_call(lambda *refs: whole_kernel(weights, *refs), out_shape=(sha...  50.2 us
    pallas_call x1, Pallas kernels, on_device(): pl.pallas_call(final_kernel, out_shape=(out, out, out), name='final', com...  2.66 us

profile of v3, /device:TPU:1, one launch (start us, length us, event | category | flops | bytes accessed | tf_op | source)
XLA Modules:
  0.0 53.5 jit_solution(13651139306250346964)
XLA Ops:
  0.6 50.2 %whole.1 = (bf16[16,2,64,128]{3,2,1,0:T(8,128)(2,1)}, bf16[16,1,64,128]{3,2,1,0:T(8,128)(2,1)}, f32[2,64,2048]{2,1,0:T(8,128)}) custom-call(bf16[64,2048]{1,0:T(8,128)(2,1)} %refs_0_.1, bf16[64,2048]{1,0:T(8,128)(2,1)} %refs_1_.1, bf16[3,1024,128]{2,1,0:T(8,128)(2,1)} %refs_2_.1, bf16[1024,128]{1,0:T(8,128)(2,1)} %refs_3_.1, ...), custom_call_target="tpu_custom_call" | custom-call | tf_op jit(solution)/shard_map/whole/pallas_call | solution.py:514
  50.9 2.7 %final.1 = (f32[64,2048]{1,0:T(8,128)}, f32[64,2048]{1,0:T(8,128)}, f32[64,2048]{1,0:T(8,128)}) custom-call(bf16[16,2,64,128]{3,2,1,0:T(8,128)(2,1)} %get-tuple-element.6.got_u, bf16[16,1,64,128]{3,2,1,0:T(8,128)(2,1)} %get-tuple-element.7.got_d, f32[2,64,2048]{2,1,0:T(8,128)} %get-tuple-element.8.local), custom_call_target="tpu_custom_call" | custom-call | tf_op jit(solution)/shard_map/final/pallas_call | solution.py:572
